TPU v7x, 512 devices: a whole 4x8x8 slice. The times are simulated.
512 devices in a mesh: ctx: 64 (over z, y), head: 8 (over x, core).
Axes of the slice: x: 4, y: 8, z: 8, core: 2. Of those that a mesh axis runs over, the one named last changes fastest.
Arguments:
- queries: bfloat16 [49152, 3072], P(('ctx', 'head')), may hold values from -20 to 20
- keys: bfloat16 [49152, 3072], P(('ctx', 'head')), may hold values from -6 to 6
- values: bfloat16 [49152, 3072], P(('ctx', 'head')), may hold values from -6 to 6
- page_blocks: int32 [64, 2], replicated, may hold values from 1 to 5, as said below
- page_links: int32 [128, 16], replicated, may hold values from 0 to 127, as said below
- global_blocks: int32 [2], replicated, may hold values from 0 to 383
Outputs:
- attended: bfloat16 [49152, 3072], P(('ctx', 'head'))
Inputs may be any that keep to these rules, and one draw needn't show every extreme that they name: `page_links`: all 32 links of the pages of one ctx index name pages of distinct other ctx indices. `page_blocks`: each row sums to 6; some ctx index has a page of exactly 5 blocks.
All inputs are finite; a program needn't handle non-finite values.
Results may differ from a plain program's by a relative error of at most 0.0048.
Values may be sent and summed in bfloat16 or wider, within the bound.
A program may use at most 128 MiB of HBM per device.

v0:
```python
import jax
import jax.numpy as jnp
from jax import lax
from jax.sharding import PartitionSpec as P

HD = 128
BLK = 128
PAGES_DEV = 2
GROWS = 64
GB = 2
masked_score = -1e30


def shards(queries, keys, values, page_blocks, page_links, global_blocks):
    q_local, k_local, v_local = (
        lax.all_to_all(queries, "head", split_axis=1, concat_axis=0, tiled=True),
        lax.all_to_all(keys, "head", split_axis=1, concat_axis=0, tiled=True),
        lax.all_to_all(values, "head", split_axis=1, concat_axis=0, tiled=True),
    )
    ctx_count = lax.axis_size("ctx")
    my_index = lax.axis_index("ctx")
    rows = q_local.shape[0]
    width = q_local.shape[1]
    n_heads = width // HD
    n_blocks = rows // BLK
    link_count = page_links.shape[1]
    my_lengths = lax.dynamic_slice_in_dim(page_blocks, my_index, 1, 0)[0]
    my_starts = jnp.cumsum(my_lengths) - my_lengths
    block_ids = jnp.arange(n_blocks, dtype=jnp.int32)
    block_page = jnp.sum((block_ids[:, None] >= my_starts[None, :]).astype(jnp.int32), axis=1) - 1
    token_page = jnp.repeat(block_page, BLK)
    pair_kv = jnp.concatenate((k_local, v_local), axis=1)
    leaders = jnp.stack(
        [
            lax.dynamic_slice_in_dim(pair_kv, my_starts[page] * BLK, BLK, 0)
            for page in range(PAGES_DEV)
        ]
    )
    reader_links = page_links.reshape(ctx_count, PAGES_DEV * link_count)
    to_mine = reader_links // PAGES_DEV == my_index
    chosen = jnp.stack(
        [
            jnp.sum((to_mine & (reader_links % PAGES_DEV == page)).astype(jnp.float32), axis=1)
            for page in range(PAGES_DEV)
        ],
        axis=1,
    )
    chosen = jnp.minimum(chosen, 1.0).astype(jnp.bfloat16)
    outgoing = jnp.einsum(
        "rp,pbf->rbf", chosen, leaders, preferred_element_type=jnp.float32
    ).astype(jnp.bfloat16)
    incoming = lax.all_to_all(outgoing, "ctx", split_axis=0, concat_axis=0, tiled=True)
    my_links = lax.dynamic_slice_in_dim(page_links, my_index * PAGES_DEV, PAGES_DEV, 0)
    sources = my_links // PAGES_DEV
    span = GROWS // GB
    owners = global_blocks // n_blocks
    places = global_blocks % n_blocks
    pieces = [
        jnp.where(
            owners[i] == my_index,
            lax.dynamic_slice_in_dim(pair_kv, places[i] * BLK, span, 0).astype(jnp.float32),
            0.0,
        )
        for i in range(GB)
    ]
    global_kv = lax.psum(jnp.concatenate(pieces, 0), "ctx").astype(jnp.bfloat16)
    scale = HD ** (-0.5)
    k_own = k_local.reshape(rows, n_heads, HD)
    v_own = v_local.reshape(rows, n_heads, HD)
    g_keys = global_kv[:, :width].reshape(GROWS, n_heads, HD)
    g_values = global_kv[:, width:].reshape(GROWS, n_heads, HD)
    group_size = 1
    for count in range(1, n_blocks + 1):
        if n_blocks % count == 0 and count * BLK <= 512:
            group_size = count
    n_groups = n_blocks // group_size
    q_groups = q_local.reshape(n_groups, group_size, BLK, n_heads, HD)
    page_groups = block_page.reshape(n_groups, group_size)

    def attend_group(operands):
        q_blocks, group_page = operands
        s_own = (
            jnp.einsum("bqhd,khd->bhqk", q_blocks, k_own, preferred_element_type=jnp.float32)
            * scale
        )
        own_mask = group_page[:, None] == token_page[None, :]
        s_own = jnp.where(own_mask[:, None, None, :], s_own, masked_score)
        s_glob = (
            jnp.einsum("bqhd,ghd->bhqg", q_blocks, g_keys, preferred_element_type=jnp.float32)
            * scale
        )
        block_kv = incoming[sources[group_page]].reshape(group_size, link_count * BLK, 2 * width)
        l_keys = block_kv[:, :, :width].reshape(group_size, link_count * BLK, n_heads, HD)
        l_values = block_kv[:, :, width:].reshape(group_size, link_count * BLK, n_heads, HD)
        s_link = (
            jnp.einsum("bqhd,bkhd->bhqk", q_blocks, l_keys, preferred_element_type=jnp.float32)
            * scale
        )
        row_max = jnp.maximum(
            jnp.maximum(jnp.max(s_own, axis=3), jnp.max(s_glob, axis=3)), jnp.max(s_link, axis=3)
        )
        w_link = jnp.exp(s_link - row_max[..., None])
        total_link = jnp.sum(w_link, axis=3)
        mixed_link = jnp.einsum(
            "bhqk,bkhd->bqhd",
            w_link.astype(jnp.bfloat16),
            l_values,
            preferred_element_type=jnp.float32,
        )
        w_own = jnp.exp(s_own - row_max[..., None])
        w_glob = jnp.exp(s_glob - row_max[..., None])
        total = jnp.sum(w_own, axis=3) + jnp.sum(w_glob, axis=3) + total_link
        mixed = jnp.einsum(
            "bhqk,khd->bqhd", w_own.astype(jnp.bfloat16), v_own, preferred_element_type=jnp.float32
        )
        mixed = mixed + jnp.einsum(
            "bhqg,ghd->bqhd",
            w_glob.astype(jnp.bfloat16),
            g_values,
            preferred_element_type=jnp.float32,
        )
        mixed = mixed + mixed_link
        mixed = mixed / jnp.transpose(total, (0, 2, 1))[..., None]
        return mixed.astype(jnp.bfloat16)

    result = lax.map(attend_group, (q_groups, page_groups)).reshape(rows, width)
    return lax.all_to_all(result, "head", split_axis=0, concat_axis=1, tiled=True)


def solution(mesh):
    return jax.shard_map(
        shards,
        mesh=mesh,
        in_specs=(
            P(("ctx", "head"), None),
            P(("ctx", "head"), None),
            P(("ctx", "head"), None),
            P(),
            P(),
            P(),
        ),
        out_specs=P(("ctx", "head"), None),
        check_vma=False,
    )
```

profile of v0, /device:TPU:256, one launch (start us, length us, event | category | flops | bytes accessed | tf_op | source)
XLA Modules:
  0.0 931.5 jit_solution(17150689993805457864)
XLA Ops:
  0.0 2.0 copy.230
  2.0 4.3 all-to-all-start.1
  6.3 1.9 copy.229
  8.2 9.1 all-to-all-done.1
  17.4 3.5 all-to-all-start.2
  21.3 0.6 fusion.66
  23.6 0.9 copy.231
  24.5 7.4 all-to-all-done.2
  31.9 3.5 all-to-all-start
  35.5 1.1 copy.179
  36.5 1.0 copy.180
  37.6 4.6 convolution_convert_fusion
  42.2 22.8 %copy.181 = bf16[64,128,768]{2,1,0:T(8,128)(2,1)} copy(bf16[64,128,768]{2,0,1:T(8,128)(2,1)S(1)} %convolution_convert_fusion) | data formatting | bytes 25165824 | tf_op jit(solution)/shard_map/convert_element_type | solution.py:51
  65.0 0.9 copy-done.5
  65.9 13.3 %all-to-all-start.3 = ((bf16[64,128,768]{2,1,0:T(8,128)(2,1)}), bf16[64,128,768]{2,1,0:T(8,128)(2,1)}, u32[]{:S(2)}, u32[]{:S(2)}) async-start(bf16[64,128,768]{2,1,0:T(8,128)(2,1)} %copy.181), calls=%async_computation.3 | async-start | bytes 25165824 | tf_op jit(solution)/shard_map/all_to_all | solution.py:52
  79.3 0.6 fusion.67
  82.4 0.5 broadcast_add_fusion
  82.9 1.3 sub.53
  84.4 708.6 %all-reduce.1 = bf16[64,768]{1,0:T(8,128)(2,1)S(1)} all-reduce(f32[64,768]{1,0:T(8,128)S(1)} %pad_maximum_fusion), channel_id=1, replica_groups=mesh['ctx'=64,'head'=8] {'ctx'}, use_global_device_ids=true, to_apply=%region_2.3 | all-reduce | flops 49152 | bytes 294912 | tf_op jit(solution)/shard_map/psum | solution.py:66
  793.1 0.6 copy.232
  793.7 0.6 copy.233
  794.5 0.9 copy.184
  795.7 0.9 copy.186
  796.8 1.0 copy.183
  797.8 112.3 %while.11 = (s32[]{:T(128)}, bf16[2,3,128,3,128]{4,2,1,3,0:T(8,128)(2,1)}, s32[2,3]{1,0:T(2,128)}, bf16[2,3,128,3,128]{4,2,1,3,0:T(8,128)(2,1)}, bf16[768,3,128]...) while((s32[]{:T(128)}, ...), condition=%wide.region_14.15_spmd.clone, body=%wide.region_7.14_spmd.clone.sunk | while | flops 1723615360 | bytes 118326752 | solution.py:126
  797.8 0.7 fusion.103
  798.4 0.7 broadcast_bitcast_fusion.2
  799.2 2.5 bitcast_reduce_fusion.2
  801.7 0.7 fusion.101
  802.4 0.6 gather_fusion
  803.0 0.6 reshape.197
  803.6 0.6 pad_clamp_fusion.5
  804.2 10.7 %gather_fusion.1 = bf16[48,128,768]{2,1,0:T(8,128)(2,1)} fusion(bf16[64,128,768]{2,1,0:T(8,128)(2,1)} %get-tuple-element.344, s32[1024]{0:T(1024)S(1)} %pad_clamp_fusion.5), kind=kCustom, calls=%fused_computation.1.clone.clone.1 | custom fusion | bytes 18874560 | tf_op jit(solution)/shard_map/while/body/eval_jaxpr/gather | solution.py:92
  814.9 8.4 fusion.102
  823.2 6.7 copy.247
  830.0 4.0 multiply_reduce_fusion.2
  834.3 3.9 fusion.105
  838.1 1.0 fusion.108
  839.2 0.6 fusion.110
  839.8 6.7 copy.249
  846.5 5.2 fusion.106
  851.7 1.0 fusion.107
  852.7 1.1 fusion.111
  853.8 0.7 fusion.103
  854.5 0.7 broadcast_bitcast_fusion.2
  855.3 2.5 bitcast_reduce_fusion.2
  857.7 0.7 fusion.101
  858.4 0.6 gather_fusion
  859.0 0.6 reshape.197
  859.6 0.6 pad_clamp_fusion.5
  860.2 10.9 %gather_fusion.1 = bf16[48,128,768]{2,1,0:T(8,128)(2,1)} fusion(bf16[64,128,768]{2,1,0:T(8,128)(2,1)} %get-tuple-element.344, s32[1024]{0:T(1024)S(1)} %pad_clamp_fusion.5), kind=kCustom, calls=%fused_computation.1.clone.clone.1 | custom fusion | bytes 18874560 | tf_op jit(solution)/shard_map/while/body/eval_jaxpr/gather | solution.py:92
  871.1 8.4 fusion.102
  879.5 6.7 copy.247
  886.2 4.0 multiply_reduce_fusion.2
  890.5 3.9 fusion.105
  894.4 1.0 fusion.108
  895.4 0.6 fusion.110
  896.0 6.7 copy.249
  902.7 5.2 fusion.106
  908.0 1.0 fusion.107
  909.0 1.1 fusion.111
  910.1 1.6 copy.188
  912.2 18.4 %all_to_all.78 = bf16[8,96,384]{2,1,0:T(8,128)(2,1)S(1)} all-to-all(bf16[8,96,384]{2,1,0:T(8,128)(2,1)S(1)} %all_to_all.69), channel_id=1, replica_groups=mesh['ctx'=64,'head'=8] {'head'}, dimensions={0} | all-to-all | bytes 1179648 | tf_op jit(solution)/shard_map/all_to_all | solution.py:127
  930.6 0.9 copy.207
  (85 shorter events, 3.3 us)
Async XLA Ops:
  0.0 20.9 %copy-start = (s32[64,2]{0,1:T(2,128)S(1)}, s32[64,2]{0,1:T(2,128)}, u32[]{:S(2)}) copy-start(s32[64,2]{0,1:T(2,128)} %param.11) | copy-start | bytes 1540
  0.0 23.1 %copy-start.13 = (s32[128,16]{0,1:T(8,128)S(1)}, s32[128,16]{0,1:T(8,128)}, u32[]{:S(2)}) copy-start(s32[128,16]{0,1:T(8,128)} %param.12) | copy-start | bytes 24580
  0.0 23.6 %copy-start.9 = (bf16[96,3072]{1,0:T(8,128)(2,1)S(1)}, bf16[96,3072]{1,0:T(8,128)(2,1)}, u32[]{:S(2)}) copy-start(bf16[96,3072]{1,0:T(8,128)(2,1)} %param.8) | copy-start | bytes 1769476
  2.0 15.4 %all-to-all-start.1 = ((bf16[96,8,384]{2,0,1:T(8,128)(2,1)}), bf16[96,8,384]{2,0,1:T(8,128)(2,1)S(1)}, u32[]{:S(2)}, u32[]{:S(2)}) async-start(bf16[96,8,384]{2,0,1:T(8,128)(2,1)} %bitcast.138), calls=%async_computation.1 | async-start | bytes 1179648 | tf_op jit(solution)/shard_map/all_to_all | solution.py:17
  17.4 14.5 %all-to-all-start.2 = ((bf16[96,8,384]{2,0,1:T(8,128)(2,1)}), bf16[96,8,384]{2,0,1:T(8,128)(2,1)S(1)}, u32[]{:S(2)}, u32[]{:S(2)}) async-start(bf16[96,8,384]{2,0,1:T(8,128)(2,1)} %bitcast.137), calls=%async_computation.2 | async-start | bytes 1179648 | tf_op jit(solution)/shard_map/all_to_all | solution.py:18
  31.9 33.1 %all-to-all-start = ((bf16[96,8,384]{2,0,1:T(8,128)(2,1)}), bf16[96,8,384]{2,0,1:T(8,128)(2,1)S(1)}, u32[]{:S(2)}, u32[]{:S(2)}) async-start(bf16[96,8,384]{2,0,1:T(8,128)(2,1)} %bitcast.139), calls=%async_computation | async-start | bytes 1179648 | tf_op jit(solution)/shard_map/all_to_all | solution.py:16
  65.0 14.2 %copy-start.14 = (s32[2]{0:T(128)S(1)}, s32[2]{0:T(128)}, u32[]{:S(2)}) copy-start(s32[2]{0:T(128)} %param.13) | copy-start | bytes 28
  65.0 0.9 copy-start.5
  65.9 731.9 %all-to-all-start.3 = ((bf16[64,128,768]{2,1,0:T(8,128)(2,1)}), bf16[64,128,768]{2,1,0:T(8,128)(2,1)}, u32[]{:S(2)}, u32[]{:S(2)}) async-start(bf16[64,128,768]{2,1,0:T(8,128)(2,1)} %copy.181), calls=%async_computation.3 | async-start | bytes 25165824 | tf_op jit(solution)/shard_map/all_to_all | solution.py:52
  79.2 717.3 %copy-start.6 = (bf16[96,8,384]{2,0,1:T(8,128)(2,1)S(1)}, bf16[96,8,384]{2,0,1:T(8,128)(2,1)}, u32[]{:S(2)}) copy-start(bf16[96,8,384]{2,0,1:T(8,128)(2,1)} %copy-done.5) | copy-start | bytes 1769476
  829.9 4.0 copy-start.2
  829.9 4.0 copy-start.7
  830.0 4.3 copy-start.8
  834.2 4.9 copy-start.3
  846.5 5.2 copy-start.10
  851.7 1.0 copy-start.4
  851.7 1.0 copy-start.11
  851.7 1.0 copy-start.12
  886.2 4.0 copy-start.2
  886.2 4.0 copy-start.7
  886.2 4.3 copy-start.8
  890.5 4.9 copy-start.3
  902.7 5.2 copy-start.10
  907.9 1.0 copy-start.4
  908.0 1.0 copy-start.11
  908.0 1.0 copy-start.12
  910.1 21.5 %copy-start.1 = (s32[64,2]{0,1:T(2,128)S(1)}, s32[64,2]{0,1:T(2,128)}, u32[]{:S(2)}) copy-start(s32[64,2]{0,1:T(2,128)} %param.11) | copy-start | bytes 1540
where the time goes:
time: 933 us; the launch traced here: 932 us
  blocking collectives  727 us (78%)
  local copies, waits for them, and re-layouts  112 us (12%)
  matrix products  32.5 us (3%)
  starting transfers between devices  24.7 us (3%)
  waiting for transfers between devices  16.5 us (2%)
  other arithmetic  15 us (2%)
    psum x1, blocking collectives, shards(): global_kv = lax.psum(jnp.concatenate(pieces, 0), 'ctx').astype(jnp.bfloat16)  709 us
    slice x4, local copies, waits for them, and re-layouts, attend_group(): block_kv[:, :, width:].reshape(group_size, link_count * BLK, n_heads, HD)  30.1 us
    convert_element_type x1, local copies, waits for them, and re-layouts, shards(): outgoing = jnp.einsum('rp,pbf->rbf', chosen, leaders, preferred_element_t...  22.8 us
    gather x2, local copies, waits for them, and re-layouts, attend_group(): incoming[sources[group_page]]  21.6 us
  transfers between devices with their start and end apart: 4, of which 2 were waited for; matrix products, arithmetic and copies ran while one was open for 4% of the time, Pallas kernels for 0%

commit v1 on v0

--- a/solution.py
+++ b/solution.py
@@ -63,7 +63,9 @@
         )
         for i in range(GB)
     ]
-    global_kv = lax.psum(jnp.concatenate(pieces, 0), "ctx").astype(jnp.bfloat16)
+    global_kv = jnp.sum(lax.all_gather(jnp.concatenate(pieces, 0), "ctx"), axis=0).astype(
+        jnp.bfloat16
+    )
     scale = HD ** (-0.5)
     k_own = k_local.reshape(rows, n_heads, HD)
     v_own = v_local.reshape(rows, n_heads, HD)

time: 933 us -> 715 us (0.77)
  the two profiles are of different devices: /device:TPU:256 before, /device:TPU:152 now
where the time goes in v1:
time: 715 us; the launch traced here: 713 us
  waiting for transfers between devices  409 us (57%)
  local copies, waits for them, and re-layouts  111 us (16%)
  blocking collectives  95.5 us (13%)
  matrix products  32.5 us (5%)
  starting transfers between devices  26.1 us (4%)
  other arithmetic  20.8 us (3%)
  between operations  17.4 us (2%)
    all_gather x1, waiting for transfers between devices, shards(): lax.all_gather(jnp.concatenate(pieces, 0), 'ctx')  372 us
    all_to_all x1, blocking collectives, shards(): lax.all_to_all(result, 'head', split_axis=0, concat_axis=1, tiled=True)  95.5 us
    slice x4, local copies, waits for them, and re-layouts, attend_group(): block_kv[:, :, width:].reshape(group_size, link_count * BLK, n_heads, HD)  30.2 us
    all_to_all x1, waiting for transfers between devices, shards(): lax.all_to_all(outgoing, 'ctx', split_axis=0, concat_axis=0, tiled=True)  23.5 us
    convert_element_type x1, local copies, waits for them, and re-layouts, shards(): outgoing = jnp.einsum('rp,pbf->rbf', chosen, leaders, preferred_element_t...  22.8 us
    gather x2, local copies, waits for them, and re-layouts, attend_group(): incoming[sources[group_page]]  21.6 us
    all_to_all x1, starting transfers between devices, shards(): lax.all_to_all(outgoing, 'ctx', split_axis=0, concat_axis=0, tiled=True)  14.7 us
  transfers between devices with their start and end apart: 5, of which 4 were waited for; matrix products, arithmetic and copies ran while one was open for 7% of the time, Pallas kernels for 0%

profile of v1, /device:TPU:152, one launch (start us, length us, event | category | flops | bytes accessed | tf_op | source)
XLA Modules:
  0.0 713.2 jit_solution(2316156941984708707)
XLA Ops:
  6.5 2.0 copy.230
  8.5 4.3 all-to-all-start.1
  13.2 1.9 copy.229
  15.1 8.8 %all-to-all-done.1 = bf16[96,8,384]{2,0,1:T(8,128)(2,1)S(1)} async-done(((bf16[96,8,384]{2,0,1:T(8,128)(2,1)}), bf16[96,8,384]{2,0,1:T(8,128)(2,1)S(1)}, u32[]{:S(2)}, u32[]{:S(2)}) %all-to-all-start.1) | async-done | bytes 589856 | tf_op jit(solution)/shard_map/all_to_all | solution.py:17
  23.9 3.5 all-to-all-start.2
  27.4 0.6 fusion.66
  29.3 0.6 fusion.67
  33.0 0.9 copy.231
  33.9 4.5 all-to-all-done.2
  38.4 3.5 all-to-all-start
  42.1 1.1 copy.179
  43.1 1.0 copy.180
  44.2 0.7 pad_maximum_fusion
  44.9 4.6 convolution_convert_fusion
  49.5 22.8 %copy.181 = bf16[64,128,768]{2,1,0:T(8,128)(2,1)} copy(bf16[64,128,768]{2,0,1:T(8,128)(2,1)S(1)} %convolution_convert_fusion) | data formatting | bytes 25165824 | tf_op jit(solution)/shard_map/convert_element_type | solution.py:51
  72.3 0.8 copy-done.5
  73.1 14.7 %all-to-all-start.3 = ((bf16[64,128,768]{2,1,0:T(8,128)(2,1)}), bf16[64,128,768]{2,1,0:T(8,128)(2,1)}, u32[]{:S(2)}, u32[]{:S(2)}) async-start(bf16[64,128,768]{2,1,0:T(8,128)(2,1)} %copy.181), calls=%async_computation.3 | async-start | bytes 25165824 | tf_op jit(solution)/shard_map/all_to_all | solution.py:52
  88.5 1.3 sub.53
  90.1 0.9 copy.184
  91.2 0.9 copy.186
  92.3 0.9 copy.183
  93.3 372.4 %all-gather.3.cloned.1.call-done = f32[4096,768]{1,0:T(8,128)} async-done(((f32[64,768]{1,0:T(8,128)}), f32[4096,768]{1,0:T(8,128)}) %all-gather.3.cloned.1.call-update) | async-done | bytes 12582928 | tf_op jit(solution)/shard_map/all_gather | solution.py:66
  465.7 5.2 reduce_sum.78
  470.9 0.6 copy.232
  471.5 0.6 copy.233
  472.1 23.5 %all-to-all-done.3 = bf16[64,128,768]{2,1,0:T(8,128)(2,1)} async-done(((bf16[64,128,768]{2,1,0:T(8,128)(2,1)}), bf16[64,128,768]{2,1,0:T(8,128)(2,1)}, u32[]{:S(2)}, u32[]{:S(2)}) %all-to-all-start.3) | async-done | bytes 12582944 | tf_op jit(solution)/shard_map/all_to_all | solution.py:52
  495.6 112.2 %while.11 = (s32[]{:T(128)}, bf16[2,3,128,3,128]{4,2,1,3,0:T(8,128)(2,1)}, s32[2,3]{1,0:T(2,128)}, bf16[2,3,128,3,128]{4,2,1,3,0:T(8,128)(2,1)}, bf16[768,3,128]...) while((s32[]{:T(128)}, ...), condition=%wide.region_14.15_spmd.clone, body=%wide.region_7.14_spmd.clone.sunk | while | flops 1723615360 | bytes 118326752 | solution.py:128
  495.6 0.6 fusion.103
  496.2 0.7 broadcast_bitcast_fusion.2
  497.0 2.5 bitcast_reduce_fusion.2
  499.5 0.6 fusion.101
  500.7 0.6 reshape.198
  501.3 0.6 pad_clamp_fusion.5
  502.0 10.7 %gather_fusion.1 = bf16[48,128,768]{2,1,0:T(8,128)(2,1)} fusion(bf16[64,128,768]{2,1,0:T(8,128)(2,1)} %get-tuple-element.344, s32[1024]{0:T(1024)S(1)} %pad_clamp_fusion.5), kind=kCustom, calls=%fused_computation.1.clone.clone.1 | custom fusion | bytes 18874560 | tf_op jit(solution)/shard_map/while/body/eval_jaxpr/gather | solution.py:94
  512.6 8.4 %fusion.102 = (bf16[3,2048,384]{2,1,0:T(8,128)(2,1)}, bf16[3,2048,384]{2,1,0:T(8,128)(2,1)}) fusion(bf16[3,2048,768]{2,1,0:T(8,128)(2,1)} %bitcast.193), kind=kLoop, calls=%fused_computation.116.clone.1 | loop fusion | bytes 18874368 | tf_op jit(solution)/shard_map/while/body/eval_jaxpr/slice | solution.py:96
  521.0 6.7 copy.247
  527.7 4.0 multiply_reduce_fusion.2
  532.0 3.9 fusion.105
  535.9 1.0 fusion.108
  536.9 0.6 fusion.110
  537.5 6.7 copy.249
  544.2 5.2 fusion.106
  549.5 1.0 fusion.107
  550.5 1.1 fusion.111
  551.6 0.6 fusion.103
  552.2 0.7 broadcast_bitcast_fusion.2
  553.0 2.5 bitcast_reduce_fusion.2
  555.5 0.6 fusion.101
  556.7 0.6 reshape.198
  557.3 0.6 pad_clamp_fusion.5
  557.9 10.9 %gather_fusion.1 = bf16[48,128,768]{2,1,0:T(8,128)(2,1)} fusion(bf16[64,128,768]{2,1,0:T(8,128)(2,1)} %get-tuple-element.344, s32[1024]{0:T(1024)S(1)} %pad_clamp_fusion.5), kind=kCustom, calls=%fused_computation.1.clone.clone.1 | custom fusion | bytes 18874560 | tf_op jit(solution)/shard_map/while/body/eval_jaxpr/gather | solution.py:94
  568.9 8.4 %fusion.102 = (bf16[3,2048,384]{2,1,0:T(8,128)(2,1)}, bf16[3,2048,384]{2,1,0:T(8,128)(2,1)}) fusion(bf16[3,2048,768]{2,1,0:T(8,128)(2,1)} %bitcast.193), kind=kLoop, calls=%fused_computation.116.clone.1 | loop fusion | bytes 18874368 | tf_op jit(solution)/shard_map/while/body/eval_jaxpr/slice | solution.py:96
  577.2 6.7 copy.247
  583.9 4.0 multiply_reduce_fusion.2
  588.2 3.9 fusion.105
  592.1 1.0 fusion.108
  593.1 0.6 fusion.110
  593.7 6.7 copy.249
  600.5 5.2 fusion.106
  605.7 1.0 fusion.107
  606.7 1.1 fusion.111
  607.8 1.6 copy.188
  609.9 95.5 %all_to_all.78 = bf16[8,96,384]{2,1,0:T(8,128)(2,1)S(1)} all-to-all(bf16[8,96,384]{2,1,0:T(8,128)(2,1)S(1)} %all_to_all.69), channel_id=1, replica_groups=mesh['ctx'=64,'head'=8] {'head'}, dimensions={0} | all-to-all | bytes 1179648 | tf_op jit(solution)/shard_map/all_to_all | solution.py:129
  705.4 0.9 copy.207
  (88 shorter events, 5.0 us)
Async XLA Ops:
  6.5 6.3 copy-start
  6.5 22.7 %copy-start.14 = (s32[2]{0:T(128)S(1)}, s32[2]{0:T(128)}, u32[]{:S(2)}) copy-start(s32[2]{0:T(128)} %param.13) | copy-start | bytes 28
  6.5 24.6 %copy-start.13 = (s32[128,16]{0,1:T(8,128)S(1)}, s32[128,16]{0,1:T(8,128)}, u32[]{:S(2)}) copy-start(s32[128,16]{0,1:T(8,128)} %param.12) | copy-start | bytes 24580
  6.5 26.5 %copy-start.9 = (bf16[96,3072]{1,0:T(8,128)(2,1)S(1)}, bf16[96,3072]{1,0:T(8,128)(2,1)}, u32[]{:S(2)}) copy-start(bf16[96,3072]{1,0:T(8,128)(2,1)} %param.8) | copy-start | bytes 1769476
  8.5 15.4 %all-to-all-start.1 = ((bf16[96,8,384]{2,0,1:T(8,128)(2,1)}), bf16[96,8,384]{2,0,1:T(8,128)(2,1)S(1)}, u32[]{:S(2)}, u32[]{:S(2)}) async-start(bf16[96,8,384]{2,0,1:T(8,128)(2,1)} %bitcast.139), calls=%async_computation.1 | async-start | bytes 1179648 | tf_op jit(solution)/shard_map/all_to_all | solution.py:17
  23.9 14.5 %all-to-all-start.2 = ((bf16[96,8,384]{2,0,1:T(8,128)(2,1)}), bf16[96,8,384]{2,0,1:T(8,128)(2,1)S(1)}, u32[]{:S(2)}, u32[]{:S(2)}) async-start(bf16[96,8,384]{2,0,1:T(8,128)(2,1)} %bitcast.138), calls=%async_computation.2 | async-start | bytes 1179648 | tf_op jit(solution)/shard_map/all_to_all | solution.py:18
  38.4 33.9 %all-to-all-start = ((bf16[96,8,384]{2,0,1:T(8,128)(2,1)}), bf16[96,8,384]{2,0,1:T(8,128)(2,1)S(1)}, u32[]{:S(2)}, u32[]{:S(2)}) async-start(bf16[96,8,384]{2,0,1:T(8,128)(2,1)} %bitcast.140), calls=%async_computation | async-start | bytes 1179648 | tf_op jit(solution)/shard_map/all_to_all | solution.py:16
  42.0 423.7 %all-gather.3.cloned.1.call-start = ((), (), s32[]{:S(2)}) async-start(), calls=%async_computation.5 | async-start | bytes 12779520 | tf_op jit(solution)/shard_map/all_gather | solution.py:66
  72.3 0.8 copy-start.5
  73.1 422.5 %all-to-all-start.3 = ((bf16[64,128,768]{2,1,0:T(8,128)(2,1)}), bf16[64,128,768]{2,1,0:T(8,128)(2,1)}, u32[]{:S(2)}, u32[]{:S(2)}) async-start(bf16[64,128,768]{2,1,0:T(8,128)(2,1)} %copy.181), calls=%async_computation.3 | async-start | bytes 25165824 | tf_op jit(solution)/shard_map/all_to_all | solution.py:52
  87.8 4.3 copy-start.6
  527.7 4.0 copy-start.2
  527.7 4.0 copy-start.7
  527.7 4.3 copy-start.8
  531.9 4.9 copy-start.3
  544.2 5.2 copy-start.10
  549.4 1.0 copy-start.4
  549.5 1.0 copy-start.11
  549.5 1.0 copy-start.12
  583.9 4.0 copy-start.2
  583.9 4.0 copy-start.7
  583.9 4.3 copy-start.8
  588.2 4.9 copy-start.3
  600.5 5.2 copy-start.10
  605.7 1.0 copy-start.4
  605.7 1.0 copy-start.11
  605.7 1.0 copy-start.12
  607.8 98.5 %copy-start.1 = (s32[64,2]{0,1:T(2,128)S(1)}, s32[64,2]{0,1:T(2,128)}, u32[]{:S(2)}) copy-start(s32[64,2]{0,1:T(2,128)} %param.11) | copy-start | bytes 1540
Sparse Core Ops, SparseCore 0:
  45.8 419.8 all-gather.2
